TPU v7x, 32 devices: a whole 2x2x4 slice. The times are simulated.
32 devices in a mesh: tgt: 16 (over z, y, core), sup: 2 (over x).
Axes of the slice: x: 2, y: 2, z: 4, core: 2. Of those that a mesh axis runs over, the one named last changes fastest.
Arguments:
- targets: bfloat16 [3584, 12288], P('tgt', 'sup'), may hold values from -6 to 6, as said below
- support: bfloat16 [128, 12288], P('sup'), may hold values from -6 to 6, as said below
- label_weights: bfloat16 [128, 1000], P('sup'), may hold values from -0.00390625 to 0.00390625
- labels: int32 [3584], P('tgt'), may hold values from 0 to 999
- first_moment: float32 [128, 12288], P('sup', 'tgt'), may hold values from -0.6 to 0.6
- second_moment: float32 [128, 12288], P('sup', 'tgt'), may hold values from 0.001 to 0.1
Outputs:
- new_support: bfloat16 [128, 12288], P('sup')
- new_first: float32 [128, 12288], P('sup', 'tgt')
- new_second: float32 [128, 12288], P('sup', 'tgt')
Inputs may be any that keep to these rules, and one draw needn't show every extreme that they name: `targets`: image pixel values. `support`: image pixel values.
All inputs are finite; a program needn't handle non-finite values.
Results may differ from a plain program's by a relative error of at most 0.0028.
Values may be sent and summed in bfloat16 or wider, within the bound.
A program may use at most 64 MiB of HBM per device.

v0:
```python
import math
import jax
import jax.numpy as jnp
from jax import lax
from jax.sharding import PartitionSpec as P

DEPTH = 3
bias_var = 0.1
learning_rate = 0.05
first_decay = 0.9
second_decay = 0.99
first_fix = 1.0 - 0.9**10
second_fix = 1.0 - 0.99**10
adam_eps = 1e-08


def tangent_kernel(cross, target_diag, support_diag):
    tangent = cross
    current = cross
    left_diag = target_diag
    right_diag = support_diag
    for _ in range(DEPTH):
        product = (1.0 + 2.0 * left_diag)[:, None] * (1.0 + 2.0 * right_diag)[None, :]
        slope = 4.0 / math.pi / jnp.sqrt(product - 4.0 * current * current)
        current = 2.0 / math.pi * jnp.arcsin(2.0 * current / jnp.sqrt(product)) + bias_var
        tangent = current + slope * tangent
        left_diag = 2.0 / math.pi * jnp.arcsin(2.0 * left_diag / (1.0 + 2.0 * left_diag)) + bias_var
        right_diag = (
            2.0 / math.pi * jnp.arcsin(2.0 * right_diag / (1.0 + 2.0 * right_diag)) + bias_var
        )
    return tangent


def row_squares(images):
    return jnp.sum(jnp.square(images.astype(jnp.float32)), axis=1)


def shards(targets, support, label_weights, labels, first_moment, second_moment):
    pixels = support.shape[1]
    target_count = targets.shape[0] * lax.axis_size("tgt")
    support_count = support.shape[0] * lax.axis_size("sup")
    class_count = label_weights.shape[1]
    support_diag = row_squares(support) / pixels + bias_var
    slabs = lax.all_to_all(support, "sup", split_axis=1, concat_axis=0, tiled=True)
    partial_cross = lax.dot_general(
        targets, slabs, (((1,), (1,)), ((), ())), preferred_element_type=jnp.float32
    )
    cross = (
        lax.psum_scatter(
            partial_cross.astype(jnp.bfloat16), "sup", scatter_dimension=1, tiled=True
        ).astype(jnp.float32)
        / pixels
        + bias_var
    )
    target_diag = lax.psum(row_squares(targets), "sup") / pixels + bias_var

    def kernel_of(cross_in, diag_in):
        return tangent_kernel(cross_in, target_diag, diag_in)

    kernel, pullback = jax.vjp(kernel_of, cross, support_diag)
    partial_pred = jnp.dot(
        kernel.astype(jnp.bfloat16), label_weights, preferred_element_type=jnp.float32
    )
    predicted = lax.psum(partial_pred.astype(jnp.bfloat16), "sup").astype(jnp.float32)
    classes = jnp.arange(class_count, dtype=jnp.int32)
    onehot = (labels[:, None] == classes[None, :]).astype(jnp.float32)
    residual = (predicted - onehot).astype(jnp.bfloat16)
    kernel_grad = lax.dot_general(
        residual, label_weights, (((1,), (1,)), ((), ())), preferred_element_type=jnp.float32
    )
    kernel_grad = kernel_grad * (
        4.0 * pixels * math.sqrt(class_count * support_count / target_count)
    )
    cross_grad, norm_grad = pullback(kernel_grad)
    cross_low = cross_grad.astype(jnp.bfloat16)
    all_grads = lax.all_gather(cross_low, "sup", axis=1, tiled=True)
    slab_grad = lax.dot_general(
        all_grads, targets, (((0,), (0,)), ((), ())), preferred_element_type=jnp.float32
    )
    image_grad = lax.all_to_all(
        slab_grad.astype(jnp.bfloat16), "sup", split_axis=0, concat_axis=1, tiled=True
    ).astype(slab_grad.dtype)
    gradient = (image_grad + 2.0 * norm_grad[:, None] * support.astype(jnp.float32)) / pixels
    shares = lax.psum_scatter(gradient, "tgt", scatter_dimension=1, tiled=True)
    slab_width = shares.shape[1]
    own_pixels = lax.dynamic_slice_in_dim(
        support, lax.axis_index("tgt") * slab_width, slab_width, 1
    ).astype(jnp.float32)
    new_first = first_decay * first_moment + (1.0 - first_decay) * shares
    new_second = second_decay * second_moment + (1.0 - second_decay) * shares * shares
    update = (
        learning_rate * (new_first / first_fix) / (jnp.sqrt(new_second / second_fix) + adam_eps)
    )
    new_slab = (own_pixels - update).astype(jnp.bfloat16)
    new_support = lax.all_gather(new_slab, "tgt", axis=1, tiled=True)
    return (new_support, new_first, new_second)


def solution(mesh):
    return jax.shard_map(
        shards,
        mesh=mesh,
        in_specs=(
            P("tgt", "sup"),
            P("sup", None),
            P("sup", None),
            P("tgt"),
            P("sup", "tgt"),
            P("sup", "tgt"),
        ),
        out_specs=(P("sup", None), P("sup", "tgt"), P("sup", "tgt")),
        check_vma=False,
    )
```

profile of v0, /device:TPU:0, one launch (start us, length us, event | category | flops | bytes accessed | tf_op | source)
XLA Modules:
  0.0 233.6 jit_solution(4970678291514561601)
XLA Ops:
  7.2 0.0 copy-start
  7.2 0.0 copy-start.1
  7.2 2.8 %copy.18 = bf16[8,2,8,6144]{3,2,0,1:T(8,128)(2,1)} copy(bf16[8,2,8,6144]{3,2,1,0:T(8,128)(2,1)} %bitcast.18) | data formatting | bytes 3145728 | tf_op jit(solution)/shard_map/all_to_all | solution.py:44
  10.0 4.6 %all-to-all-start = ((bf16[64,2,6144]{2,0,1:T(8,128)(2,1)}), bf16[64,2,6144]{2,0,1:T(8,128)(2,1)}, u32[]{:S(2)}, u32[]{:S(2)}) async-start(bf16[64,2,6144]{2,0,1:T(8,128)(2,1)} %bitcast.20), calls=%async_computation | async-start | bytes 3145728 | tf_op jit(solution)/shard_map/all_to_all | solution.py:44
  14.6 0.0 reduce-scatter.3.cloned.1.call-start
  14.7 0.0 copy-done.1
  14.7 0.6 multiply_reduce_fusion
  15.3 20.2 %psum.14 = f32[224]{0:T(256)S(1)} all-reduce(f32[224]{0:T(256)S(1)} %multiply_reduce_fusion), channel_id=1, replica_groups=mesh['tgt'=16,'sup'=2] {'sup'}, use_global_device_ids=true, to_apply=%region_1.0 | all-reduce | flops 224 | bytes 1792 | tf_op jit(solution)/shard_map/psum | solution.py:55
  35.5 1.8 fusion
  37.3 0.1 broadcast_add_fusion
  37.4 0.1 multiply_add_fusion.6
  37.5 0.1 broadcast_add_fusion.2
  37.5 0.0 all-to-all-done
  37.5 0.0 copy-start.6
  37.6 3.1 %convolution_convert_fusion.2 = bf16[224,128]{0,1:T(8,128)(2,1)} fusion(bf16[224,6144]{1,0:T(8,128)(2,1)S(1)} %copy-done.1, bf16[128,6144]{1,0:T(8,128)(2,1)} %bitcast.1), kind=kOutput, calls=%fused_computation.10 | convolution fusion | flops 352350208 | bytes 4382720 | tf_op jit(solution)/shard_map/dot_general | solution.py:45
  40.7 0.0 reduce-scatter.3.cloned.1.call-update
  40.7 0.0 all-reduce.2.cloned.1.call-start
  40.8 0.1 multiply_add_fusion.7
  40.8 10.6 %reduce-scatter.3.cloned.1.call-done = bf16[224,64]{0,1:T(8,128)(2,1)} async-done(((bf16[224,128]{0,1:T(8,128)(2,1)}), bf16[224,64]{0,1:T(8,128)(2,1)}) %reduce-scatter.3.cloned.1.call-update) | async-done | bytes 28688 | tf_op jit(solution)/shard_map/reduce_scatter | solution.py:49
  51.4 0.0 copy-start.5
  51.4 0.0 copy-done
  51.4 2.6 %convolution_convert_fusion.1 = bf16[224,1000]{1,0:T(8,128)(2,1)} fusion(bf16[64,1000]{1,0:T(8,128)(2,1)S(1)} %copy-done, f32[64]{0:T(128)S(1)} %multiply_add_fusion.7, f32[224]{0:T(256)S(1)} %multiply_add_fusion.6, f32[64]{0:T(128)S(1)} %get-tuple-element.13, f32[224]{0:T(256)S(1)} %get-tuple-element.11, ...), kind=kOutput, calls=%fused_computation.9 | convolution fusion | flops 29641472 | bytes 608128 | tf_op jit(solution)/shard_map/dot_general | solution.py:61
  54.0 0.0 all-reduce.2.cloned.1.call-update
  54.0 27.5 %all-reduce.2.cloned.1.call-done = bf16[224,1000]{1,0:T(8,128)(2,1)} async-done(((bf16[224,1000]{1,0:T(8,128)(2,1)}), bf16[224,1000]{1,0:T(8,128)(2,1)}) %all-reduce.2.cloned.1.call-update) | async-done | bytes 448016 | tf_op jit(solution)/shard_map/psum | solution.py:64
  81.6 0.0 copy-done.6
  81.6 0.0 copy-done.5
  81.6 1.8 fusion.52
  83.4 0.8 fusion.63
  84.1 0.2 fusion.60
  84.3 4.6 %all_gather.6 = bf16[224,128]{0,1:T(8,128)(2,1)S(1)} all-gather(bf16[224,64]{0,1:T(8,128)(2,1)S(1)} %fusion.60), channel_id=1, replica_groups=mesh['tgt'=16,'sup'=2] {'sup'}, dimensions={1}, use_global_device_ids=true | all-gather | bytes 86016 | tf_op jit(solution)/shard_map/all_gather | solution.py:76
  88.9 1.7 convolution_convert_fusion
  90.6 3.7 %all-to-all-start.1 = ((bf16[2,64,6144]{2,1,0:T(8,128)(2,1)}), bf16[2,64,6144]{2,1,0:T(8,128)(2,1)S(1)}, u32[]{:S(2)}, u32[]{:S(2)}) async-start(bf16[2,64,6144]{2,1,0:T(8,128)(2,1)} %bitcast.21), calls=%async_computation.2 | async-start | bytes 3145728 | tf_op jit(solution)/shard_map/all_to_all | solution.py:80
  94.3 0.0 reduce-scatter.5.cloned.1.call-start
  94.4 18.1 %all-to-all-done.1 = bf16[2,64,6144]{2,1,0:T(8,128)(2,1)S(1)} async-done(((bf16[2,64,6144]{2,1,0:T(8,128)(2,1)}), bf16[2,64,6144]{2,1,0:T(8,128)(2,1)S(1)}, u32[]{:S(2)}, u32[]{:S(2)}) %all-to-all-start.1) | async-done | bytes 1572896 | tf_op jit(solution)/shard_map/all_to_all | solution.py:80
  112.5 0.3 convert_bitcast_fusion
  112.8 0.0 copy-start.2
  112.8 0.2 copy.16
  113.0 1.2 copy-done.2
  114.2 2.2 fusion.2
  116.4 0.0 copy-start.3
  116.4 0.0 copy-start.4
  116.4 0.0 reduce-scatter.5.cloned.1.call-update
  116.4 0.0 all-gather.2.cloned.1.call-start
  116.5 66.4 %reduce-scatter.5.cloned.1.call-done = f32[64,768]{1,0:T(8,128)} async-done(((f32[64,12288]{1,0:T(8,128)}), f32[64,768]{1,0:T(8,128)}) %reduce-scatter.5.cloned.1.call-update) | async-done | bytes 196624 | tf_op jit(solution)/shard_map/reduce_scatter | solution.py:84
  182.9 0.0 copy-done.3
  182.9 0.0 copy-done.4
  182.9 1.8 subtract_convert_fusion.2
  184.6 0.0 all-gather.2.cloned.1.call-update
  184.7 39.7 %all-gather.2.cloned.1.call-done = bf16[64,12288]{1,0:T(8,128)(2,1)} async-done(((bf16[64,768]{1,0:T(8,128)(2,1)}), bf16[64,12288]{1,0:T(8,128)(2,1)}) %all-gather.2.cloned.1.call-update) | async-done | bytes 1572880 | tf_op jit(solution)/shard_map/all_gather | solution.py:95
  224.4 2.7 %copy.21 = bf16[64,12288]{1,0:T(8,128)(2,1)} copy(bf16[64,12288]{1,0:T(8,128)(2,1)} %all-gather.2.cloned.1.call-done) | data formatting | bytes 3145728
  (1 shorter events, 0.0 us)
Async XLA Ops:
  7.2 44.3 %copy-start = (bf16[64,1000]{1,0:T(8,128)(2,1)S(1)}, bf16[64,1000]{1,0:T(8,128)(2,1)}, u32[]{:S(2)}) copy-start(bf16[64,1000]{1,0:T(8,128)(2,1)} %param.8) | copy-start | bytes 384004
  7.2 7.5 %copy-start.1 = (bf16[224,6144]{1,0:T(8,128)(2,1)S(1)}, bf16[224,6144]{1,0:T(8,128)(2,1)}, u32[]{:S(2)}) copy-start(bf16[224,6144]{1,0:T(8,128)(2,1)} %param.6) | copy-start | bytes 8257540
  10.0 27.5 %all-to-all-start = ((bf16[64,2,6144]{2,0,1:T(8,128)(2,1)}), bf16[64,2,6144]{2,0,1:T(8,128)(2,1)}, u32[]{:S(2)}, u32[]{:S(2)}) async-start(bf16[64,2,6144]{2,0,1:T(8,128)(2,1)} %bitcast.20), calls=%async_computation | async-start | bytes 3145728 | tf_op jit(solution)/shard_map/all_to_all | solution.py:44
  14.6 36.8 %reduce-scatter.3.cloned.1.call-start = ((), (), s32[]{:S(2)}) async-start(), calls=%async_computation.4 | async-start | bytes 98304 | tf_op jit(solution)/shard_map/reduce_scatter | solution.py:49
  37.5 44.0 %copy-start.6 = (s32[224]{0:T(256)S(1)}, s32[224]{0:T(256)}, u32[]{:S(2)}) copy-start(s32[224]{0:T(256)} %param.9) | copy-start | bytes 2692
  40.7 40.9 %all-reduce.2.cloned.1.call-start = ((), (), s32[]{:S(2)}) async-start(), calls=%async_computation.5 | async-start | bytes 917504 | tf_op jit(solution)/shard_map/psum | solution.py:64
  51.4 30.2 %copy-start.5 = (bf16[224,64]{0,1:T(8,128)(2,1)S(1)}, bf16[224,64]{0,1:T(8,128)(2,1)}, u32[]{:S(2)}) copy-start(bf16[224,64]{0,1:T(8,128)(2,1)} %reduce-scatter.3.cloned.1.call-done) | copy-start | bytes 86020
  90.6 21.8 %all-to-all-start.1 = ((bf16[2,64,6144]{2,1,0:T(8,128)(2,1)}), bf16[2,64,6144]{2,1,0:T(8,128)(2,1)S(1)}, u32[]{:S(2)}, u32[]{:S(2)}) async-start(bf16[2,64,6144]{2,1,0:T(8,128)(2,1)} %bitcast.21), calls=%async_computation.2 | async-start | bytes 3145728 | tf_op jit(solution)/shard_map/all_to_all | solution.py:80
  94.3 88.5 %reduce-scatter.5.cloned.1.call-start = ((), (), s32[]{:S(2)}) async-start(), calls=%async_computation.6 | async-start | bytes 3342336 | tf_op jit(solution)/shard_map/reduce_scatter | solution.py:84
  112.8 1.4 copy-start.2
  116.4 66.5 %copy-start.3 = (f32[64,768]{1,0:T(8,128)S(1)}, f32[64,768]{1,0:T(8,128)}, u32[]{:S(2)}) copy-start(f32[64,768]{1,0:T(8,128)} %param.10) | copy-start | bytes 589828
  116.4 66.5 %copy-start.4 = (f32[64,768]{1,0:T(8,128)S(1)}, f32[64,768]{1,0:T(8,128)}, u32[]{:S(2)}) copy-start(f32[64,768]{1,0:T(8,128)} %param.11) | copy-start | bytes 589828
  116.4 108.0 %all-gather.2.cloned.1.call-start = ((), (), s32[]{:S(2)}) async-start(), calls=%async_computation.7 | async-start | bytes 1671168 | tf_op jit(solution)/shard_map/all_gather | solution.py:95
Sparse Core Ops, SparseCore 0:
  40.8 10.5 reduce-scatter.2
  54.3 27.2 all-reduce.1
  116.5 66.2 reduce-scatter.4
  185.5 38.8 all-gather.1
where the time goes:
time: 234 us
  waiting for transfers between devices  162 us (69%)
  blocking collectives  24.8 us (11%)
  between operations  13.9 us (6%)
  matrix products  9.22 us (4%)
  starting transfers between devices  8.44 us (4%)
  other arithmetic  7.9 us (3%)
  local copies, waits for them, and re-layouts  6.92 us (3%)
    reduce_scatter x1, waiting for transfers between devices, shards(): shares = lax.psum_scatter(gradient, 'tgt', scatter_dimension=1, tiled=True)  66.4 us
    all_gather x1, waiting for transfers between devices, shards(): new_support = lax.all_gather(new_slab, 'tgt', axis=1, tiled=True)  39.7 us
    psum x1, waiting for transfers between devices, shards(): lax.psum(partial_pred.astype(jnp.bfloat16), 'sup').astype(jnp.float32)  27.5 us
    psum x1, blocking collectives, shards(): target_diag = lax.psum(row_squares(targets), 'sup') / pixels + bias_var  20.2 us
    all_to_all x1, waiting for transfers between devices, shards(): lax.all_to_all(slab_grad.astype(jnp.bfloat16), 'sup', split_axis=0, conca...  18.1 us
    reduce_scatter x1, waiting for transfers between devices, shards(): lax.psum_scatter(partial_cross.astype(jnp.bfloat16), 'sup', scatter_dimen...  10.6 us
  transfers between devices with their start and end apart: 6, of which 5 were waited for; matrix products, arithmetic and copies ran while one was open for 1% of the time, Pallas kernels for 0%

commit v1 on v0

--- a/solution.py
+++ b/solution.py
@@ -92,7 +92,29 @@
         learning_rate * (new_first / first_fix) / (jnp.sqrt(new_second / second_fix) + adam_eps)
     )
     new_slab = (own_pixels - update).astype(jnp.bfloat16)
-    new_support = lax.all_gather(new_slab, "tgt", axis=1, tiled=True)
+    local_out, upper, heard = (lax.axis_size("tgt"), lax.axis_index("tgt"), new_slab.shape[1])
+    by_rank = []
+    for no in range(local_out):
+        by_rank.append((no, (no + 1) % local_out))
+    gallery = []
+    for no in range(local_out):
+        gallery.append((no, (no - 1) % local_out))
+    new_support = jnp.zeros(
+        (*new_slab.shape[:1], local_out * heard, *new_slab.shape[2:]), new_slab.dtype
+    )
+    new_support = lax.dynamic_update_slice_in_dim(new_support, new_slab, upper * heard, axis=1)
+    t1 = local_out // 2
+    kept_arr = parts_out = new_slab
+    for dev_i in range(1, t1 + 1):
+        kept_arr = lax.ppermute(kept_arr, "tgt", by_rank)
+        new_support = lax.dynamic_update_slice_in_dim(
+            new_support, kept_arr, (upper - dev_i) % local_out * heard, axis=1
+        )
+        if dev_i < local_out - t1:
+            parts_out = lax.ppermute(parts_out, "tgt", gallery)
+            new_support = lax.dynamic_update_slice_in_dim(
+                new_support, parts_out, (upper + dev_i) % local_out * heard, axis=1
+            )
     return (new_support, new_first, new_second)
 
 

time: 234 us -> 248 us (1.060)
  starting transfers between devices: 8.44 us -> 40.5 us
  waiting for transfers between devices: 162 us -> 145 us
    all_gather x1 -> x0, waiting for transfers between devices: 39.7 us -> none  [shards(): new_support = lax.all_gather(new_slab, 'tgt', axis=1, tiled=True)]
    ppermute x0 -> x15, starting transfers between devices: none -> 31.8 us  [the longest x7 31.8 us: shards(): parts_out = lax.ppermute(parts_out, 'tgt', gallery)]
    ppermute x0 -> x15, waiting for transfers between devices: none -> 22.3 us  [the longest x8 21.8 us: shards(): kept_arr = lax.ppermute(kept_arr, 'tgt', by_rank)]
  transfers between devices with their start and end apart: 6 -> 20, of which waited for: 5 -> 16; matrix products, arithmetic and copies ran while one was open for 1% -> 1% of each run, Pallas kernels for 0% -> 0%
where the time goes in v1:
time: 248 us
  waiting for transfers between devices  145 us (58%)
  starting transfers between devices  40.5 us (16%)
  blocking collectives  24.8 us (10%)
  between operations  14 us (6%)
  matrix products  9.22 us (4%)
  other arithmetic  7.88 us (3%)
  local copies, waits for them, and re-layouts  6.38 us (3%)
    reduce_scatter x1, waiting for transfers between devices, shards(): shares = lax.psum_scatter(gradient, 'tgt', scatter_dimension=1, tiled=True)  66.4 us
    ppermute x7, starting transfers between devices, shards(): parts_out = lax.ppermute(parts_out, 'tgt', gallery)  31.8 us
    psum x1, waiting for transfers between devices, shards(): lax.psum(partial_pred.astype(jnp.bfloat16), 'sup').astype(jnp.float32)  27.5 us
    ppermute x8, waiting for transfers between devices, shards(): kept_arr = lax.ppermute(kept_arr, 'tgt', by_rank)  21.8 us
    psum x1, blocking collectives, shards(): target_diag = lax.psum(row_squares(targets), 'sup') / pixels + bias_var  20.2 us
    all_to_all x1, waiting for transfers between devices, shards(): lax.all_to_all(slab_grad.astype(jnp.bfloat16), 'sup', split_axis=0, conca...  18.1 us
    reduce_scatter x1, waiting for transfers between devices, shards(): lax.psum_scatter(partial_cross.astype(jnp.bfloat16), 'sup', scatter_dimen...  10.6 us
  transfers between devices with their start and end apart: 20, of which 16 were waited for; matrix products, arithmetic and copies ran while one was open for 1% of the time, Pallas kernels for 0%

profile of v1, /device:TPU:0, one launch (start us, length us, event | category | flops | bytes accessed | tf_op | source)
XLA Modules:
  0.0 247.7 jit_solution(11171423584132606758)
XLA Ops:
  7.2 0.0 copy-start
  7.2 2.7 %copy.18 = bf16[8,2,8,6144]{3,2,0,1:T(8,128)(2,1)} copy(bf16[8,2,8,6144]{3,2,1,0:T(8,128)(2,1)} %bitcast.18) | data formatting | bytes 3145728 | tf_op jit(solution)/shard_map/all_to_all | solution.py:44
  9.9 4.9 %all-to-all-start = ((bf16[64,2,6144]{2,0,1:T(8,128)(2,1)}), bf16[64,2,6144]{2,0,1:T(8,128)(2,1)}, u32[]{:S(2)}, u32[]{:S(2)}) async-start(bf16[64,2,6144]{2,0,1:T(8,128)(2,1)} %bitcast.20), calls=%async_computation | async-start | bytes 3145728 | tf_op jit(solution)/shard_map/all_to_all | solution.py:44
  14.8 0.0 reduce-scatter.3.cloned.1.call-start
  14.9 0.6 multiply_reduce_fusion
  15.5 20.2 %psum.14 = f32[224]{0:T(256)S(1)} all-reduce(f32[224]{0:T(256)S(1)} %multiply_reduce_fusion), channel_id=1, replica_groups=mesh['tgt'=16,'sup'=2] {'sup'}, use_global_device_ids=true, to_apply=%region_1.0 | all-reduce | flops 224 | bytes 1792 | tf_op jit(solution)/shard_map/psum | solution.py:55
  35.7 1.8 fusion
  37.5 0.1 broadcast_add_fusion
  37.6 0.1 multiply_add_fusion.6
  37.6 0.1 broadcast_add_fusion.2
  37.7 3.1 %convolution_convert_fusion.2 = bf16[224,128]{0,1:T(8,128)(2,1)} fusion(bf16[224,6144]{1,0:T(8,128)(2,1)S(1)} %copy-done.1, bf16[128,6144]{1,0:T(8,128)(2,1)} %bitcast.1), kind=kOutput, calls=%fused_computation.10 | convolution fusion | flops 352350208 | bytes 4382720 | tf_op jit(solution)/shard_map/dot_general | solution.py:45
  40.8 0.0 reduce-scatter.3.cloned.1.call-update
  40.9 0.0 all-reduce.2.cloned.1.call-start
  40.9 0.1 multiply_add_fusion.7
  41.0 10.6 %reduce-scatter.3.cloned.1.call-done = bf16[224,64]{0,1:T(8,128)(2,1)} async-done(((bf16[224,128]{0,1:T(8,128)(2,1)}), bf16[224,64]{0,1:T(8,128)(2,1)}) %reduce-scatter.3.cloned.1.call-update) | async-done | bytes 28688 | tf_op jit(solution)/shard_map/reduce_scatter | solution.py:49
  51.6 2.6 %convolution_convert_fusion.1 = bf16[224,1000]{1,0:T(8,128)(2,1)} fusion(bf16[64,1000]{1,0:T(8,128)(2,1)S(1)} %copy-done, f32[64]{0:T(128)S(1)} %multiply_add_fusion.7, f32[224]{0:T(256)S(1)} %multiply_add_fusion.6, f32[64]{0:T(128)S(1)} %get-tuple-element.14, f32[224]{0:T(256)S(1)} %get-tuple-element.12, ...), kind=kOutput, calls=%fused_computation.9 | convolution fusion | flops 29641472 | bytes 608128 | tf_op jit(solution)/shard_map/dot_general | solution.py:61
  54.2 0.0 all-reduce.2.cloned.1.call-update
  54.2 27.5 %all-reduce.2.cloned.1.call-done = bf16[224,1000]{1,0:T(8,128)(2,1)} async-done(((bf16[224,1000]{1,0:T(8,128)(2,1)}), bf16[224,1000]{1,0:T(8,128)(2,1)}) %all-reduce.2.cloned.1.call-update) | async-done | bytes 448016 | tf_op jit(solution)/shard_map/psum | solution.py:64
  81.7 1.8 fusion.52
  83.5 0.8 fusion.63
  84.3 0.2 fusion.60
  84.5 4.6 %all_gather.3 = bf16[224,128]{0,1:T(8,128)(2,1)S(1)} all-gather(bf16[224,64]{0,1:T(8,128)(2,1)S(1)} %fusion.60), channel_id=1, replica_groups=mesh['tgt'=16,'sup'=2] {'sup'}, dimensions={1}, use_global_device_ids=true | all-gather | bytes 86016 | tf_op jit(solution)/shard_map/all_gather | solution.py:76
  89.1 1.7 convolution_convert_fusion
  90.8 3.7 %all-to-all-start.1 = ((bf16[2,64,6144]{2,1,0:T(8,128)(2,1)}), bf16[2,64,6144]{2,1,0:T(8,128)(2,1)S(1)}, u32[]{:S(2)}, u32[]{:S(2)}) async-start(bf16[2,64,6144]{2,1,0:T(8,128)(2,1)} %bitcast.21), calls=%async_computation.2 | async-start | bytes 3145728 | tf_op jit(solution)/shard_map/all_to_all | solution.py:80
  94.5 0.0 reduce-scatter.5.cloned.1.call-start
  94.6 18.1 %all-to-all-done.1 = bf16[2,64,6144]{2,1,0:T(8,128)(2,1)S(1)} async-done(((bf16[2,64,6144]{2,1,0:T(8,128)(2,1)}), bf16[2,64,6144]{2,1,0:T(8,128)(2,1)S(1)}, u32[]{:S(2)}, u32[]{:S(2)}) %all-to-all-start.1) | async-done | bytes 1572896 | tf_op jit(solution)/shard_map/all_to_all | solution.py:80
  112.6 0.3 convert_bitcast_fusion
  112.9 0.0 copy-start.2
  113.0 0.2 copy.16
  113.2 1.2 copy-done.2
  114.4 2.2 fusion.2
  116.5 0.0 reduce-scatter.5.cloned.1.call-update
  116.5 0.0 copy-start.4
  116.6 66.4 %reduce-scatter.5.cloned.1.call-done = f32[64,768]{1,0:T(8,128)} async-done(((f32[64,12288]{1,0:T(8,128)}), f32[64,768]{1,0:T(8,128)}) %reduce-scatter.5.cloned.1.call-update) | async-done | bytes 196624 | tf_op jit(solution)/shard_map/reduce_scatter | solution.py:84
  183.0 0.1 broadcast_in_dim.2
  183.1 0.8 copy-done.5
  183.9 1.8 constant_dynamic-update-slice_fusion.15
  185.7 0.0 collective-permute-start
  185.7 4.4 %collective-permute-start.1 = (bf16[64,768]{1,0:T(8,128)(2,1)}, bf16[64,768]{1,0:T(8,128)(2,1)S(1)}, u32[]{:S(2)}, u32[]{:S(2)}) collective-permute-start(bf16[64,768]{1,0:T(8,128)(2,1)} %get-tuple-element.7), channel_id=1, source_target_pairs={{0,30},{2,0},{4,2},{6,4},{8,6},{10,8},{12,10},{14,12},{16,14},{18,... | collective-permute-start | bytes 294920 | tf_op jit(solution)/shard_map/ppermute | solution.py:114
  190.1 2.5 %collective-permute-done = bf16[64,768]{1,0:T(8,128)(2,1)S(1)} collective-permute-done((bf16[64,768]{1,0:T(8,128)(2,1)}, bf16[64,768]{1,0:T(8,128)(2,1)S(1)}, u32[]{:S(2)}, u32[]{:S(2)}) %collective-permute-start) | collective-permute-done | bytes 98336 | tf_op jit(solution)/shard_map/ppermute | solution.py:109
  192.6 0.0 collective-permute-start.2
  192.6 0.0 collective-permute-done.1
  192.7 4.4 %collective-permute-start.3 = (bf16[64,768]{1,0:T(8,128)(2,1)S(1)}, bf16[64,768]{1,0:T(8,128)(2,1)S(1)}, u32[]{:S(2)}, u32[]{:S(2)}) collective-permute-start(bf16[64,768]{1,0:T(8,128)(2,1)S(1)} %collective-permute-done.1), channel_id=1, source_target_pairs={{0,30},{2,0},{4,2},{6,4},{8,6},{10,8},{12,10},{14,12},{16,14},{18,... | collective-permute-start | bytes 294920 | tf_op jit(solution)/shard_map/ppermute | solution.py:114
  197.1 2.3 collective-permute-done.2
  199.4 0.0 collective-permute-start.4
  199.4 0.0 collective-permute-done.3
  199.4 4.5 %collective-permute-start.5 = (bf16[64,768]{1,0:T(8,128)(2,1)S(1)}, bf16[64,768]{1,0:T(8,128)(2,1)S(1)}, u32[]{:S(2)}, u32[]{:S(2)}) collective-permute-start(bf16[64,768]{1,0:T(8,128)(2,1)S(1)} %collective-permute-done.3), channel_id=1, source_target_pairs={{0,30},{2,0},{4,2},{6,4},{8,6},{10,8},{12,10},{14,12},{16,14},{18,... | collective-permute-start | bytes 294920 | tf_op jit(solution)/shard_map/ppermute | solution.py:114
  204.0 2.2 collective-permute-done.4
  206.2 0.0 collective-permute-start.6
  206.2 4.6 %collective-permute-start.7 = (bf16[64,768]{1,0:T(8,128)(2,1)S(1)}, bf16[64,768]{1,0:T(8,128)(2,1)S(1)}, u32[]{:S(2)}, u32[]{:S(2)}) collective-permute-start(bf16[64,768]{1,0:T(8,128)(2,1)S(1)} %collective-permute-done.5), channel_id=1, source_target_pairs={{0,30},{2,0},{4,2},{6,4},{8,6},{10,8},{12,10},{14,12},{16,14},{18,... | collective-permute-start | bytes 294920 | tf_op jit(solution)/shard_map/ppermute | solution.py:114
  210.8 2.1 collective-permute-done.6
  212.9 0.1 collective-permute-done.7
  213.0 4.6 %collective-permute-start.9 = (bf16[64,768]{1,0:T(8,128)(2,1)S(1)}, bf16[64,768]{1,0:T(8,128)(2,1)S(1)}, u32[]{:S(2)}, u32[]{:S(2)}) collective-permute-start(bf16[64,768]{1,0:T(8,128)(2,1)S(1)} %collective-permute-done.7), channel_id=1, source_target_pairs={{0,30},{2,0},{4,2},{6,4},{8,6},{10,8},{12,10},{14,12},{16,14},{18,... | collective-permute-start | bytes 294920 | tf_op jit(solution)/shard_map/ppermute | solution.py:114
  217.6 2.1 collective-permute-done.8
  219.7 0.1 collective-permute-done.9
  219.8 4.6 %collective-permute-start.11 = (bf16[64,768]{1,0:T(8,128)(2,1)S(1)}, bf16[64,768]{1,0:T(8,128)(2,1)S(1)}, u32[]{:S(2)}, u32[]{:S(2)}) collective-permute-start(bf16[64,768]{1,0:T(8,128)(2,1)S(1)} %collective-permute-done.9), channel_id=1, source_target_pairs={{0,30},{2,0},{4,2},{6,4},{8,6},{10,8},{12,10},{14,12},{16,14},{18,... | collective-permute-start | bytes 294920 | tf_op jit(solution)/shard_map/ppermute | solution.py:114
  224.5 2.1 collective-permute-done.10
  226.5 0.1 collective-permute-done.11
  226.7 4.6 %collective-permute-start.13 = (bf16[64,768]{1,0:T(8,128)(2,1)S(1)}, bf16[64,768]{1,0:T(8,128)(2,1)S(1)}, u32[]{:S(2)}, u32[]{:S(2)}) collective-permute-start(bf16[64,768]{1,0:T(8,128)(2,1)S(1)} %collective-permute-done.11), channel_id=1, source_target_pairs={{0,30},{2,0},{4,2},{6,4},{8,6},{10,8},{12,10},{14,12},{16,14},{18,... | collective-permute-start | bytes 294920 | tf_op jit(solution)/shard_map/ppermute | solution.py:114
  231.3 2.0 collective-permute-done.12
  233.3 0.2 collective-permute-done.13
  233.5 6.5 %collective-permute-done.14 = bf16[64,768]{1,0:T(8,128)(2,1)S(1)} collective-permute-done((bf16[64,768]{1,0:T(8,128)(2,1)S(1)}, bf16[64,768]{1,0:T(8,128)(2,1)S(1)}, u32[]{:S(2)}, u32[]{:S(2)}) %collective-permute-start.14) | collective-permute-done | bytes 98336 | tf_op jit(solution)/shard_map/ppermute | solution.py:109
  240.0 0.0 copy-start.3
  240.1 1.1 copy-done.3
  (31 shorter events, 0.2 us)
Async XLA Ops:
  7.2 44.4 %copy-start = (bf16[64,1000]{1,0:T(8,128)(2,1)S(1)}, bf16[64,1000]{1,0:T(8,128)(2,1)}, u32[]{:S(2)}) copy-start(bf16[64,1000]{1,0:T(8,128)(2,1)} %param.8) | copy-start | bytes 384004
  9.9 5.0 %copy-start.1 = (bf16[224,6144]{1,0:T(8,128)(2,1)S(1)}, bf16[224,6144]{1,0:T(8,128)(2,1)}, u32[]{:S(2)}) copy-start(bf16[224,6144]{1,0:T(8,128)(2,1)} %param.6) | copy-start | bytes 8257540
  9.9 27.8 %all-to-all-start = ((bf16[64,2,6144]{2,0,1:T(8,128)(2,1)}), bf16[64,2,6144]{2,0,1:T(8,128)(2,1)}, u32[]{:S(2)}, u32[]{:S(2)}) async-start(bf16[64,2,6144]{2,0,1:T(8,128)(2,1)} %bitcast.20), calls=%async_computation | async-start | bytes 3145728 | tf_op jit(solution)/shard_map/all_to_all | solution.py:44
  14.8 36.8 %reduce-scatter.3.cloned.1.call-start = ((), (), s32[]{:S(2)}) async-start(), calls=%async_computation.4 | async-start | bytes 98304 | tf_op jit(solution)/shard_map/reduce_scatter | solution.py:49
  40.8 40.9 %copy-start.7 = (s32[224]{0:T(256)S(1)}, s32[224]{0:T(256)}, u32[]{:S(2)}) copy-start(s32[224]{0:T(256)} %param.9) | copy-start | bytes 2692
  40.9 40.9 %all-reduce.2.cloned.1.call-start = ((), (), s32[]{:S(2)}) async-start(), calls=%async_computation.5 | async-start | bytes 917504 | tf_op jit(solution)/shard_map/psum | solution.py:64
  51.6 30.2 %copy-start.6 = (bf16[224,64]{0,1:T(8,128)(2,1)S(1)}, bf16[224,64]{0,1:T(8,128)(2,1)}, u32[]{:S(2)}) copy-start(bf16[224,64]{0,1:T(8,128)(2,1)} %reduce-scatter.3.cloned.1.call-done) | copy-start | bytes 86020
  90.8 21.8 %all-to-all-start.1 = ((bf16[2,64,6144]{2,1,0:T(8,128)(2,1)}), bf16[2,64,6144]{2,1,0:T(8,128)(2,1)S(1)}, u32[]{:S(2)}, u32[]{:S(2)}) async-start(bf16[2,64,6144]{2,1,0:T(8,128)(2,1)} %bitcast.21), calls=%async_computation.2 | async-start | bytes 3145728 | tf_op jit(solution)/shard_map/all_to_all | solution.py:80
  94.5 88.5 %reduce-scatter.5.cloned.1.call-start = ((), (), s32[]{:S(2)}) async-start(), calls=%async_computation.6 | async-start | bytes 3342336 | tf_op jit(solution)/shard_map/reduce_scatter | solution.py:84
  112.9 1.4 copy-start.2
  116.5 66.6 %copy-start.4 = (f32[64,768]{1,0:T(8,128)S(1)}, f32[64,768]{1,0:T(8,128)}, u32[]{:S(2)}) copy-start(f32[64,768]{1,0:T(8,128)} %param.10) | copy-start | bytes 589828
  183.0 0.9 copy-start.5
  185.7 6.9 %collective-permute-start = (bf16[64,768]{1,0:T(8,128)(2,1)}, bf16[64,768]{1,0:T(8,128)(2,1)S(1)}, u32[]{:S(2)}, u32[]{:S(2)}) collective-permute-start(bf16[64,768]{1,0:T(8,128)(2,1)} %get-tuple-element.7), channel_id=1, source_target_pairs={{0,2},{2,4},{4,6},{6,8},{8,10},{10,12},{12,14},{14,16},{16,18},{18... | collective-permute-start | bytes 294920 | tf_op jit(solution)/shard_map/ppermute | solution.py:109
  185.7 7.0 %collective-permute-start.1 = (bf16[64,768]{1,0:T(8,128)(2,1)}, bf16[64,768]{1,0:T(8,128)(2,1)S(1)}, u32[]{:S(2)}, u32[]{:S(2)}) collective-permute-start(bf16[64,768]{1,0:T(8,128)(2,1)} %get-tuple-element.7), channel_id=1, source_target_pairs={{0,30},{2,0},{4,2},{6,4},{8,6},{10,8},{12,10},{14,12},{16,14},{18,... | collective-permute-start | bytes 294920 | tf_op jit(solution)/shard_map/ppermute | solution.py:114
  192.6 6.8 %collective-permute-start.2 = (bf16[64,768]{1,0:T(8,128)(2,1)S(1)}, bf16[64,768]{1,0:T(8,128)(2,1)S(1)}, u32[]{:S(2)}, u32[]{:S(2)}) collective-permute-start(bf16[64,768]{1,0:T(8,128)(2,1)S(1)} %collective-permute-done), channel_id=1, source_target_pairs={{0,2},{2,4},{4,6},{6,8},{8,10},{10,12},{12,14},{14,16},{16,18},{18... | collective-permute-start | bytes 294920 | tf_op jit(solution)/shard_map/ppermute | solution.py:109
  192.7 6.8 %collective-permute-start.3 = (bf16[64,768]{1,0:T(8,128)(2,1)S(1)}, bf16[64,768]{1,0:T(8,128)(2,1)S(1)}, u32[]{:S(2)}, u32[]{:S(2)}) collective-permute-start(bf16[64,768]{1,0:T(8,128)(2,1)S(1)} %collective-permute-done.1), channel_id=1, source_target_pairs={{0,30},{2,0},{4,2},{6,4},{8,6},{10,8},{12,10},{14,12},{16,14},{18,... | collective-permute-start | bytes 294920 | tf_op jit(solution)/shard_map/ppermute | solution.py:114
  199.4 6.7 %collective-permute-start.4 = (bf16[64,768]{1,0:T(8,128)(2,1)S(1)}, bf16[64,768]{1,0:T(8,128)(2,1)S(1)}, u32[]{:S(2)}, u32[]{:S(2)}) collective-permute-start(bf16[64,768]{1,0:T(8,128)(2,1)S(1)} %collective-permute-done.2), channel_id=1, source_target_pairs={{0,2},{2,4},{4,6},{6,8},{8,10},{10,12},{12,14},{14,16},{16,18},{18... | collective-permute-start | bytes 294920 | tf_op jit(solution)/shard_map/ppermute | solution.py:109
  199.4 6.7 %collective-permute-start.5 = (bf16[64,768]{1,0:T(8,128)(2,1)S(1)}, bf16[64,768]{1,0:T(8,128)(2,1)S(1)}, u32[]{:S(2)}, u32[]{:S(2)}) collective-permute-start(bf16[64,768]{1,0:T(8,128)(2,1)S(1)} %collective-permute-done.3), channel_id=1, source_target_pairs={{0,30},{2,0},{4,2},{6,4},{8,6},{10,8},{12,10},{14,12},{16,14},{18,... | collective-permute-start | bytes 294920 | tf_op jit(solution)/shard_map/ppermute | solution.py:114
  206.2 6.7 %collective-permute-start.6 = (bf16[64,768]{1,0:T(8,128)(2,1)S(1)}, bf16[64,768]{1,0:T(8,128)(2,1)S(1)}, u32[]{:S(2)}, u32[]{:S(2)}) collective-permute-start(bf16[64,768]{1,0:T(8,128)(2,1)S(1)} %collective-permute-done.4), channel_id=1, source_target_pairs={{0,2},{2,4},{4,6},{6,8},{8,10},{10,12},{12,14},{14,16},{16,18},{18... | collective-permute-start | bytes 294920 | tf_op jit(solution)/shard_map/ppermute | solution.py:109
  206.2 6.8 %collective-permute-start.7 = (bf16[64,768]{1,0:T(8,128)(2,1)S(1)}, bf16[64,768]{1,0:T(8,128)(2,1)S(1)}, u32[]{:S(2)}, u32[]{:S(2)}) collective-permute-start(bf16[64,768]{1,0:T(8,128)(2,1)S(1)} %collective-permute-done.5), channel_id=1, source_target_pairs={{0,30},{2,0},{4,2},{6,4},{8,6},{10,8},{12,10},{14,12},{16,14},{18,... | collective-permute-start | bytes 294920 | tf_op jit(solution)/shard_map/ppermute | solution.py:114
  212.9 6.8 %collective-permute-start.8 = (bf16[64,768]{1,0:T(8,128)(2,1)S(1)}, bf16[64,768]{1,0:T(8,128)(2,1)S(1)}, u32[]{:S(2)}, u32[]{:S(2)}) collective-permute-start(bf16[64,768]{1,0:T(8,128)(2,1)S(1)} %collective-permute-done.6), channel_id=1, source_target_pairs={{0,2},{2,4},{4,6},{6,8},{8,10},{10,12},{12,14},{14,16},{16,18},{18... | collective-permute-start | bytes 294920 | tf_op jit(solution)/shard_map/ppermute | solution.py:109
  213.0 6.8 %collective-permute-start.9 = (bf16[64,768]{1,0:T(8,128)(2,1)S(1)}, bf16[64,768]{1,0:T(8,128)(2,1)S(1)}, u32[]{:S(2)}, u32[]{:S(2)}) collective-permute-start(bf16[64,768]{1,0:T(8,128)(2,1)S(1)} %collective-permute-done.7), channel_id=1, source_target_pairs={{0,30},{2,0},{4,2},{6,4},{8,6},{10,8},{12,10},{14,12},{16,14},{18,... | collective-permute-start | bytes 294920 | tf_op jit(solution)/shard_map/ppermute | solution.py:114
  219.7 6.8 %collective-permute-start.10 = (bf16[64,768]{1,0:T(8,128)(2,1)S(1)}, bf16[64,768]{1,0:T(8,128)(2,1)S(1)}, u32[]{:S(2)}, u32[]{:S(2)}) collective-permute-start(bf16[64,768]{1,0:T(8,128)(2,1)S(1)} %collective-permute-done.8), channel_id=1, source_target_pairs={{0,2},{2,4},{4,6},{6,8},{8,10},{10,12},{12,14},{14,16},{16,18},{18... | collective-permute-start | bytes 294920 | tf_op jit(solution)/shard_map/ppermute | solution.py:109
  219.8 6.8 %collective-permute-start.11 = (bf16[64,768]{1,0:T(8,128)(2,1)S(1)}, bf16[64,768]{1,0:T(8,128)(2,1)S(1)}, u32[]{:S(2)}, u32[]{:S(2)}) collective-permute-start(bf16[64,768]{1,0:T(8,128)(2,1)S(1)} %collective-permute-done.9), channel_id=1, source_target_pairs={{0,30},{2,0},{4,2},{6,4},{8,6},{10,8},{12,10},{14,12},{16,14},{18,... | collective-permute-start | bytes 294920 | tf_op jit(solution)/shard_map/ppermute | solution.py:114
  226.5 6.7 %collective-permute-start.12 = (bf16[64,768]{1,0:T(8,128)(2,1)S(1)}, bf16[64,768]{1,0:T(8,128)(2,1)S(1)}, u32[]{:S(2)}, u32[]{:S(2)}) collective-permute-start(bf16[64,768]{1,0:T(8,128)(2,1)S(1)} %collective-permute-done.10), channel_id=1, source_target_pairs={{0,2},{2,4},{4,6},{6,8},{8,10},{10,12},{12,14},{14,16},{16,18},{18... | collective-permute-start | bytes 294920 | tf_op jit(solution)/shard_map/ppermute | solution.py:109
  226.7 6.8 %collective-permute-start.13 = (bf16[64,768]{1,0:T(8,128)(2,1)S(1)}, bf16[64,768]{1,0:T(8,128)(2,1)S(1)}, u32[]{:S(2)}, u32[]{:S(2)}) collective-permute-start(bf16[64,768]{1,0:T(8,128)(2,1)S(1)} %collective-permute-done.11), channel_id=1, source_target_pairs={{0,30},{2,0},{4,2},{6,4},{8,6},{10,8},{12,10},{14,12},{16,14},{18,... | collective-permute-start | bytes 294920 | tf_op jit(solution)/shard_map/ppermute | solution.py:114
  233.3 6.7 %collective-permute-start.14 = (bf16[64,768]{1,0:T(8,128)(2,1)S(1)}, bf16[64,768]{1,0:T(8,128)(2,1)S(1)}, u32[]{:S(2)}, u32[]{:S(2)}) collective-permute-start(bf16[64,768]{1,0:T(8,128)(2,1)S(1)} %collective-permute-done.12), channel_id=1, source_target_pairs={{0,2},{2,4},{4,6},{6,8},{8,10},{10,12},{12,14},{14,16},{16,18},{18... | collective-permute-start | bytes 294920 | tf_op jit(solution)/shard_map/ppermute | solution.py:109
  240.0 1.1 copy-start.3
Sparse Core Ops, SparseCore 0:
  41.0 10.5 reduce-scatter.2
  54.5 27.2 all-reduce.1
  116.7 66.2 reduce-scatter.4
